TPU v7x, 32 devices: a whole 2x2x4 slice. The times are simulated.
32 devices in a mesh: ab: 16 (over z, y, core), ij: 2 (over x).
Axes of the slice: x: 2, y: 2, z: 4, core: 2. Of those that a mesh axis runs over, the one named last changes fastest.
Arguments:
- amplitudes: float32 [128, 2048], P('ab', 'ij'), may hold values from -6 to 6
- integrals: float32 [16384, 2048], P('ab'), may hold values from -0.125 to 0.125
- occ_pairs: float32 [128], P(('ab', 'ij')), may hold values from -2 to -0.5
- vir_pairs: float32 [16384], P('ab'), may hold values from 1 to 4
Outputs:
- update: float32 [128, 16384], P(('ab', 'ij'))
All inputs are finite; a program needn't handle non-finite values.
Results may differ from a plain program's by a relative error of at most 0.00007.
Values sent between devices are 32-bit elements; how exact they have to be, the bound alone decides.
No kernel may reach another device: no remote copies, remote signals or barrier semaphores. Data moves between devices by JAX's collectives and lax.ppermute only.
A program may use at most 64 MiB of HBM per device.

v0:
```python
import jax
import jax.numpy as jnp
from jax import lax
from jax.sharding import PartitionSpec as P


def contract(block_amps, integrals):
    return lax.dot_general(
        block_amps,
        integrals,
        (((1,), (1,)), ((), ())),
        precision=lax.Precision.HIGHEST,
        preferred_element_type=jnp.float32,
    )


def shards(amplitudes, integrals, occ_pairs, vir_pairs):
    arrived = lax.all_to_all(amplitudes, "ij", split_axis=0, concat_axis=1, tiled=True)
    slice_amps = lax.all_gather(arrived, "ab", axis=0, tiled=True)
    row_energy = lax.all_gather(occ_pairs, "ab", axis=0, tiled=True)
    groups = lax.axis_size("ab")
    per_device = occ_pairs.shape[0]
    panel_cols = integrals.shape[1]
    grouped = slice_amps.reshape(groups, per_device, panel_cols)
    energy_grouped = row_energy.reshape(groups, per_device)
    block_amps = grouped.reshape(-1, panel_cols)
    residual = contract(block_amps, integrals)
    block_energy = energy_grouped.reshape(-1)
    residual = residual / (vir_pairs[None, :] - block_energy[:, None])
    moved = lax.all_to_all(residual, "ab", split_axis=0, concat_axis=1, tiled=True)
    return moved


def solution(mesh):
    return jax.shard_map(
        shards,
        mesh=mesh,
        in_specs=(P("ab", "ij"), P("ab", None), P(("ab", "ij")), P("ab")),
        out_specs=P(("ab", "ij"), None),
        check_vma=False,
    )
```

profile of v0, /device:TPU:0, one launch (start us, length us, event | category | flops | bytes accessed | tf_op | source)
XLA Modules:
  0.0 86.3 jit_solution(3729236758331604290)
XLA Ops:
  0.0 1.4 %all_to_all.28 = f32[2,4,1024]{2,1,0:T(4,128)} reshape(f32[8,1024]{1,0:T(8,128)} %param.4) | data formatting | bytes 65536 | tf_op jit(solution)/shard_map/all_to_all | solution.py:18
  1.4 4.2 %all-to-all-start = ((f32[2,4,1024]{2,1,0:T(4,128)}), f32[2,4,1024]{2,1,0:T(4,128)S(1)}, u32[]{:S(2)}, u32[]{:S(2)}) async-start(f32[2,4,1024]{2,1,0:T(4,128)} %all_to_all.28), calls=%async_computation | async-start | bytes 65536 | tf_op jit(solution)/shard_map/all_to_all | solution.py:18
  5.6 1.3 %dynamic-slice = u32[1]{0:T(128)} dynamic-slice(u32[32]{0:T(128)} %constant.4, u32[]{:T(128)S(6)} %add), dynamic_slice_sizes={1} | dynamic-slice | bytes 12
  7.6 0.9 dynamic-update-slice
  8.5 34.0 %all-reduce = f32[64]{0:T(128)S(1)} all-reduce(f32[64]{0:T(128)S(1)} %dynamic-update-slice), channel_id=1, replica_groups=mesh['ab'=16,'ij'=2] {'ab'}, use_global_device_ids=true, to_apply=%add | all-reduce | flops 64 | bytes 512
  42.5 0.0 all-to-all-done
  42.5 18.7 %all-gather = f32[16,4,2048]{2,1,0:T(4,128)S(1)} all-gather(f32[1,4,2048]{2,1,0:T(4,128)S(1)} %bitcast.10), channel_id=1, replica_groups=mesh['ab'=16,'ij'=2] {'ab'}, dimensions={0}, use_global_device_ids=true | all-gather | bytes 557056 | tf_op jit(solution)/shard_map/all_gather | solution.py:19
  61.2 0.2 reshape.12
  61.4 10.5 %convolution_divide_fusion = f32[64,1024]{1,0:T(8,128)S(1)} fusion(f32[64,2048]{1,0:T(8,128)S(1)} %reshape.12, f32[1024,2048]{1,0:T(8,128)} %param.5, f32[64]{0:T(128)S(1)} %all-reduce, f32[1024]{0:T(1024)} %param.7), kind=kOutput, calls=%fused_computation | convolution fusion | flops 1610743808 | bytes 9179392 | tf_op jit(solution)/shard_map/dot_general | solution.py:8
  71.9 0.1 all_to_all.32
  72.0 13.6 %all_to_all.38 = f32[16,4,1024]{2,1,0:T(4,128)S(1)} all-to-all(f32[16,4,1024]{2,1,0:T(4,128)S(1)} %all_to_all.32), channel_id=1, replica_groups=mesh['ab'=16,'ij'=2] {'ab'}, dimensions={0} | all-to-all | bytes 524288 | tf_op jit(solution)/shard_map/all_to_all | solution.py:30
  85.6 0.7 copy.11
  (1 shorter events, 0.0 us)
Async XLA Ops:
  1.4 41.1 %all-to-all-start = ((f32[2,4,1024]{2,1,0:T(4,128)}), f32[2,4,1024]{2,1,0:T(4,128)S(1)}, u32[]{:S(2)}, u32[]{:S(2)}) async-start(f32[2,4,1024]{2,1,0:T(4,128)} %all_to_all.28), calls=%async_computation | async-start | bytes 65536 | tf_op jit(solution)/shard_map/all_to_all | solution.py:18
where the time goes:
time: 86.6 us; the launch traced here: 86.3 us
  blocking collectives  66.3 us (77%)
  matrix products  10.5 us (12%)
  local copies, waits for them, and re-layouts  4.52 us (5%)
  starting transfers between devices  4.23 us (5%)
    unnamed x1, blocking collectives  34 us
    all_gather x1, blocking collectives, shards(): slice_amps = lax.all_gather(arrived, 'ab', axis=0, tiled=True)  18.7 us
    all_to_all x1, blocking collectives, shards(): lax.all_to_all(residual, 'ab', split_axis=0, concat_axis=1, tiled=True)  13.6 us
    dot_general x1, matrix products, contract(): lax.dot_general(block_amps, integrals, (((1,), (1,)), ((), ())), precisio...  10.5 us
    all_to_all x1, starting transfers between devices, shards(): lax.all_to_all(amplitudes, 'ij', split_axis=0, concat_axis=1, tiled=True)  4.23 us
    unnamed x5, local copies, waits for them, and re-layouts  3.06 us
  transfers between devices with their start and end apart: 1, of which 0 were waited for; matrix products, arithmetic and copies ran while one was open for 3% of the time, Pallas kernels for 0%

commit v1 on v0

v1 whole, which is shorter than its diff:
```python
import functools
import itertools

import jax
import jax.numpy as jnp
from jax import lax
from jax.experimental import pallas as pl
from jax.experimental.pallas import tpu as pltpu
from jax.sharding import Mesh, PartitionSpec as P

LANES = 128
NT = (((1,), (1,)), ((), ()))
VMEM = pl.BlockSpec(memory_space=pltpu.VMEM)


def limit(mib):
    return pltpu.CompilerParams(vmem_limit_bytes=mib * 1024 * 1024)


def is_power(n):
    return n & (n - 1) == 0


def target(i, d, n):
    return i ^ d if is_power(n) else (i + d) % n


def source(i, d, n):
    return i ^ d if is_power(n) else (i + n - d) % n


def send(x, axes, distance):
    sizes = [lax.axis_size(a) for a in axes]
    pairs = []
    for at in itertools.product(*(range(n) for n in sizes)):
        to = [target(i, d, n) for i, d, n in zip(at, distance, sizes)]
        s = t = 0
        for n, i, j in zip(sizes, at, to):
            s, t = s * n + i, t * n + j
        pairs.append((s, t))
    return lax.ppermute(x, axes, pairs)


def split(x):
    hi = x.astype(jnp.bfloat16)
    return hi, (x - hi.astype(jnp.float32)).astype(jnp.bfloat16)


def dot(a, b):
    return lax.dot_general(a, b, NT, preferred_element_type=jnp.float32)


def split_kernel(chunk, integrals_ref, hi_ref, lo_ref, landed, sems):
    starts = range(0, landed.shape[0], chunk)
    copies = [
        pltpu.make_async_copy(
            integrals_ref.at[pl.ds(start, chunk)], landed.at[pl.ds(start, chunk)], sems.at[i]
        )
        for i, start in enumerate(starts)
    ]
    for copy in copies:
        copy.start()
    for copy, start in zip(copies, starts):
        copy.wait()
        part = slice(start, start + chunk)
        hi_ref[part, :], lo_ref[part, :] = split(landed[part, :])


def split_integrals(integrals):
    panel, cols = integrals.shape
    chunk = min(128, panel)
    return pl.pallas_call(
        functools.partial(split_kernel, chunk),
        out_shape=[jax.ShapeDtypeStruct((panel, cols), jnp.bfloat16)] * 2,
        in_specs=[pl.BlockSpec(memory_space=pltpu.HBM)],
        out_specs=[VMEM] * 2,
        scratch_shapes=[
            pltpu.VMEM((panel, cols), jnp.float32),
            pltpu.SemaphoreType.DMA((panel // chunk,)),
        ],
        compiler_params=limit(42),
        cost_estimate=pl.CostEstimate(
            flops=3 * panel * cols, bytes_accessed=8 * panel * cols, transcendentals=0
        ),
        name="split_integrals",
    )(integrals)


def pack_kernel(amplitudes_ref, occ_ref, out_ref):
    slices, per, width = out_ref.shape
    cols = width - LANES
    for s in range(slices):
        out_ref[s, :, :cols] = amplitudes_ref[s * per : (s + 1) * per, :]
        for row in range(per):
            out_ref[s, row, cols:] = jnp.full((LANES,), occ_ref[row], jnp.float32)


def pack(amplitudes, occ_pairs):
    rows, cols = amplitudes.shape
    per = occ_pairs.shape[0]
    return pl.pallas_call(
        pack_kernel,
        out_shape=jax.ShapeDtypeStruct((rows // per, per, cols + LANES), jnp.float32),
        in_specs=[VMEM, pl.BlockSpec(memory_space=pltpu.SMEM)],
        out_specs=VMEM,
        name="pack",
    )(amplitudes, occ_pairs)


def sort_kernel(axis, *refs):
    *block_refs, _, out_ref = refs
    slices = out_ref.shape[0]
    me = lax.axis_index(axis)
    for d in range(slices):
        for k, ref in enumerate(block_refs):
            out_ref[d, k] = ref[target(me, d, slices)]


def sort_slices(blocks, after):
    slices, per, width = blocks[0].shape
    return pl.pallas_call(
        functools.partial(sort_kernel, "ij"),
        out_shape=jax.ShapeDtypeStruct((slices, len(blocks), per, width), jnp.float32),
        in_specs=[VMEM] * len(blocks) + [pl.BlockSpec(memory_space=pl.ANY)],
        out_specs=VMEM,
        compiler_params=limit(8),
        name="sort_slices",
    )(*blocks, after)


def contract_kernel(keys, chunk, *refs):
    *piece_refs, hi_ref, lo_ref, vir_ref, out_ref, amps = refs
    outer, inner, cores, per, panel = out_ref.shape
    slices = hi_ref.shape[1] // (piece_refs[0].shape[2] - LANES)
    cols = hi_ref.shape[1] // slices
    at = [lax.axis_index(a) for a in ("outer", "inner", "core", "ij")]
    rows = amps.shape[0] // 2
    group = outer * per
    energy = [None] * (rows // group)
    for (core, near, part), ref in zip(keys, piece_refs):
        base = (core * inner + near) * group
        hi, lo = split(ref[:, :, :cols].reshape(group, cols))
        where = pl.ds(pl.multiple_of(source(at[3], part, slices) * cols, LANES), cols)
        amps[base : base + group, where] = hi
        amps[rows + base : rows + base + group, where] = lo
        if part == 0:
            energy[base // group] = ref[:, :, cols:].reshape(group, LANES)
    energy = jnp.concatenate(energy, axis=0)[:, :1]
    for start in range(0, panel, chunk):
        some = slice(start, start + chunk)
        wide = dot(amps[...], hi_ref[some, :])
        residual = wide[:rows] + (wide[rows:] + dot(amps[:rows, :], lo_ref[some, :]))
        update = residual / (vir_ref[:, some] - energy)
        update = update.reshape(cores, inner, outer, per, chunk)
        for c, n, o in itertools.product(range(cores), range(inner), range(outer)):
            out_ref[
                source(at[0], o, outer), source(at[1], n, inner), source(at[2], c, cores), :, some
            ] = update[c, n, o]


def contract(pieces, hi, lo, vir_pairs, inner, cores):
    keys = sorted(pieces)
    outer, per, width = pieces[keys[0]].shape
    panel, cols = hi.shape
    rows = outer * inner * cores * per
    return pl.pallas_call(
        functools.partial(contract_kernel, keys, min(256, panel)),
        out_shape=jax.ShapeDtypeStruct((outer, inner, cores, per, panel), jnp.float32),
        in_specs=[VMEM] * (len(keys) + 3),
        out_specs=VMEM,
        scratch_shapes=[pltpu.VMEM((2 * rows, cols), jnp.bfloat16)],
        compiler_params=limit(32),
        cost_estimate=pl.CostEstimate(
            flops=6 * rows * panel * cols,
            bytes_accessed=4 * (panel * cols + rows * cols + rows * panel),
            transcendentals=0,
        ),
        name="contract",
    )(*(pieces[k] for k in keys), hi, lo, vir_pairs)


def shards(amplitudes, integrals, occ_pairs, vir_pairs):
    outer, inner, cores, slices = (lax.axis_size(a) for a in ("outer", "inner", "core", "ij"))
    per, panel = occ_pairs.shape[0], integrals.shape[0]
    own = pack(amplitudes, occ_pairs)
    far = [own] + [send(own, ("outer",), (d,)) for d in range(1, outer)]
    hi, lo = split_integrals(integrals)
    near = sort_slices(far, hi)
    pieces = {}
    for n, s in itertools.product(range(inner), range(slices)):
        piece = near[s]
        if n or s:
            piece = send(piece, ("inner", "ij"), (n, s))
        pieces[0, n, s] = piece
        for c in range(1, cores):
            pieces[c, n, s] = send(piece, ("core",), (c,))
    update = contract(pieces, hi, lo, vir_pairs[None, :], inner, cores)
    groups = outer * inner * cores
    update = update.reshape(groups, per, panel)
    moved = lax.all_to_all(
        update, ("outer", "inner", "core"), split_axis=0, concat_axis=0, tiled=True
    )
    return moved.transpose(1, 0, 2).reshape(per, groups * panel)


def solution(mesh):
    groups, slices = mesh.devices.shape
    cores = 2 if groups % 2 == 0 else 1
    chips = groups // cores
    outer = chips
    if is_power(chips):
        outer = 1 << (chips.bit_length() // 2)
    shape = (outer, chips // outer, cores, slices)
    ab = ("outer", "inner", "core")
    return jax.shard_map(
        shards,
        mesh=Mesh(mesh.devices.reshape(shape), (*ab, "ij")),
        in_specs=(P(ab, "ij"), P(ab, None), P((*ab, "ij")), P(ab)),
        out_specs=P((*ab, "ij"), None),
        check_vma=False,
    )
```

time: 86.6 us -> 38.3 us (0.44)
  blocking collectives: 66.3 us -> 14.2 us
  matrix products: 10.5 us -> 0 us
  Pallas kernels: 0 us -> 7.9 us
  waiting for transfers between devices: 0.01 us -> 5.96 us
  starting transfers between devices: 4.23 us -> 9.21 us
  local copies, waits for them, and re-layouts: 4.52 us -> 0.73 us
    unnamed x1 -> x0, blocking collectives: 34 us -> none
    all_gather x1 -> x0, blocking collectives: 18.7 us -> none  [shards(): slice_amps = lax.all_gather(arrived, 'ab', axis=0, tiled=True)]
    dot_general x1 -> x0, matrix products: 10.5 us -> none  [contract(): lax.dot_general(block_amps, integrals, (((1,), (1,)), ((), ())), precisio...]
    ppermute x0 -> x10, starting transfers between devices: none -> 9.21 us  [send(): return lax.ppermute(x, axes, pairs)]
    pallas_call x0 -> x4, Pallas kernels: none -> 7.9 us  [the longest x1 3.61 us: split_integrals(): pl.pallas_call(functools.partial(split_kernel, chunk), out_shape=[jax.Sha...]
    ppermute x0 -> x10, waiting for transfers between devices: none -> 5.96 us  [send(): return lax.ppermute(x, axes, pairs)]
    all_to_all x1 -> x0, starting transfers between devices: 4.23 us -> none  [shards(): lax.all_to_all(amplitudes, 'ij', split_axis=0, concat_axis=1, tiled=True)]
    unnamed x5, local copies, waits for them, and re-layouts: 3.06 us -> 0.71 us
  transfers between devices with their start and end apart: 1 -> 10, of which waited for: 0 -> 6; matrix products, arithmetic and copies ran while one was open for 3% -> 0% of each run, Pallas kernels for 0% -> 10%
where the time goes in v1:
time: 38.3 us; the launch traced here: 38 us
  blocking collectives  14.2 us (37%)
  starting transfers between devices  9.21 us (24%)
  Pallas kernels  7.9 us (21%)
  waiting for transfers between devices  5.96 us (16%)
  local copies, waits for them, and re-layouts  0.73 us (2%)
    all_to_all x1, blocking collectives, shards(): lax.all_to_all(update, ('outer', 'inner', 'core'), split_axis=0, concat_a...  14.2 us
    ppermute x10, starting transfers between devices, send(): return lax.ppermute(x, axes, pairs)  9.21 us
    ppermute x10, waiting for transfers between devices, send(): return lax.ppermute(x, axes, pairs)  5.96 us
    pallas_call x1, Pallas kernels, split_integrals(): pl.pallas_call(functools.partial(split_kernel, chunk), out_shape=[jax.Sha...  3.61 us
    pallas_call x1, Pallas kernels, contract(): pl.pallas_call(functools.partial(contract_kernel, keys, min(256, panel)),...  2.86 us
    pallas_call x1, Pallas kernels, pack(): pl.pallas_call(pack_kernel, out_shape=jax.ShapeDtypeStruct((rows // per,...  1.42 us
  transfers between devices with their start and end apart: 10, of which 6 were waited for; matrix products, arithmetic and copies ran while one was open for 0% of the time, Pallas kernels for 10%

profile of v1, /device:TPU:0, one launch (start us, length us, event | category | flops | bytes accessed | tf_op | source)
XLA Modules:
  0.0 38.0 jit_solution(3014799767965684546)
XLA Ops:
  0.0 1.4 %pack.1.refs_0_ = f32[2,4,1152]{2,1,0:T(4,128)} custom-call(f32[8,1024]{1,0:T(8,128)} %amplitudes_ref.1, f32[4]{0:T(128)} %occ_ref.1), custom_call_target="tpu_custom_call" | custom-call | tf_op jit(solution)/shard_map/pack/pallas_call | solution.py:101
  1.4 5.1 %collective-permute-start.2 = (f32[2,4,1152]{2,1,0:T(4,128)}, f32[2,4,1152]{2,1,0:T(4,128)S(1)}, u32[]{:S(2)}, u32[]{:S(2)}) collective-permute-start(f32[2,4,1152]{2,1,0:T(4,128)} %pack.1.refs_0_), channel_id=1, source_target_pairs={{0,24},{8,16},{16,8},{24,0},{1,25},{9,17},{17,9},{25,1},{2,26},{10... | collective-permute-start | bytes 110600 | tf_op jit(solution)/shard_map/ppermute | solution.py:41
  6.5 0.0 collective-permute-start.1
  6.5 0.6 %collective-permute-start = (f32[2,4,1152]{2,1,0:T(4,128)}, f32[2,4,1152]{2,1,0:T(4,128)S(1)}, u32[]{:S(2)}, u32[]{:S(2)}) collective-permute-start(f32[2,4,1152]{2,1,0:T(4,128)} %pack.1.refs_0_), channel_id=1, source_target_pairs={{0,8},{8,0},{16,24},{24,16},{1,9},{9,1},{17,25},{25,17},{2,10},{10... | collective-permute-start | bytes 110600 | tf_op jit(solution)/shard_map/ppermute | solution.py:41
  7.1 3.6 %split_integrals.1 = (bf16[1024,2048]{1,0:T(8,128)(2,1)S(1)}, bf16[1024,2048]{1,0:T(8,128)(2,1)S(1)}) custom-call(f32[1024,2048]{1,0:T(8,128)} %integrals_ref.1), custom_call_target="tpu_custom_call" | custom-call | flops 6291456 | bytes 16777216 | tf_op jit(solution)/shard_map/split_integrals/pallas_call | solution.py:72
  10.7 0.0 copy-start.1
  10.7 0.0 collective-permute-done.2.refs_3_
  10.7 0.9 %collective-permute-done.1.refs_2_ = f32[2,4,1152]{2,1,0:T(4,128)S(1)} collective-permute-done((f32[2,4,1152]{2,1,0:T(4,128)}, f32[2,4,1152]{2,1,0:T(4,128)S(1)}, u32[]{:S(2)}, u32[]{:S(2)}) %collective-permute-start.1) | collective-permute-done | bytes 36896 | tf_op jit(solution)/shard_map/ppermute | solution.py:41
  11.6 0.0 collective-permute-done.refs_1_
  11.6 2.5 %collective-permute-start.5 = (f32[4,4,1152]{2,1,0:T(4,128)S(1)}, f32[4,4,1152]{2,1,0:T(4,128)S(1)}, u32[]{:S(2)}, u32[]{:S(2)}) collective-permute-start(f32[4,4,1152]{2,1,0:T(4,128)S(1)} %get-tuple-element.9), channel_id=1, source_target_pairs={{0,5},{1,4},{4,1},{5,0},{2,7},{3,6},{6,3},{7,2},{8,13},{9,12},{12,... | collective-permute-start | bytes 221192 | tf_op jit(solution)/shard_map/ppermute | solution.py:41
  14.1 0.5 %collective-permute-start.3 = (f32[4,4,1152]{2,1,0:T(4,128)S(1)}, f32[4,4,1152]{2,1,0:T(4,128)S(1)}, u32[]{:S(2)}, u32[]{:S(2)}) collective-permute-start(f32[4,4,1152]{2,1,0:T(4,128)S(1)} %get-tuple-element.9), channel_id=1, source_target_pairs={{0,1},{1,0},{4,5},{5,4},{2,3},{3,2},{6,7},{7,6},{8,9},{9,8},{12,13... | collective-permute-start | bytes 221192 | tf_op jit(solution)/shard_map/ppermute | solution.py:41
  14.7 0.5 %collective-permute-start.4 = (f32[4,4,1152]{2,1,0:T(4,128)S(1)}, f32[4,4,1152]{2,1,0:T(4,128)S(1)}, u32[]{:S(2)}, u32[]{:S(2)}) collective-permute-start(f32[4,4,1152]{2,1,0:T(4,128)S(1)} %get-tuple-element.10.refs_0_), channel_id=1, source_target_pairs={{0,4},{1,5},{4,0},{5,1},{2,6},{3,7},{6,2},{7,3},{8,12},{9,13},{12,... | collective-permute-start | bytes 221192 | tf_op jit(solution)/shard_map/ppermute | solution.py:41
  15.2 0.0 collective-permute-start.6
  15.2 1.8 %collective-permute-done.5.refs_3_ = f32[4,4,1152]{2,1,0:T(4,128)S(1)} collective-permute-done((f32[4,4,1152]{2,1,0:T(4,128)S(1)}, f32[4,4,1152]{2,1,0:T(4,128)S(1)}, u32[]{:S(2)}, u32[]{:S(2)}) %collective-permute-start.5) | collective-permute-done | bytes 73760 | tf_op jit(solution)/shard_map/ppermute | solution.py:41
  16.9 0.0 collective-permute-start.9
  16.9 1.5 %collective-permute-done.3.refs_1_ = f32[4,4,1152]{2,1,0:T(4,128)S(1)} collective-permute-done((f32[4,4,1152]{2,1,0:T(4,128)S(1)}, f32[4,4,1152]{2,1,0:T(4,128)S(1)}, u32[]{:S(2)}, u32[]{:S(2)}) %collective-permute-start.3) | collective-permute-done | bytes 73760 | tf_op jit(solution)/shard_map/ppermute | solution.py:41
  18.5 0.0 collective-permute-start.7
  18.5 0.5 %collective-permute-done.4.refs_2_ = f32[4,4,1152]{2,1,0:T(4,128)S(1)} collective-permute-done((f32[4,4,1152]{2,1,0:T(4,128)S(1)}, f32[4,4,1152]{2,1,0:T(4,128)S(1)}, u32[]{:S(2)}, u32[]{:S(2)}) %collective-permute-start.4) | collective-permute-done | bytes 73760 | tf_op jit(solution)/shard_map/ppermute | solution.py:41
  19.0 0.0 collective-permute-start.8
  19.0 0.7 %collective-permute-done.7.refs_5_ = f32[4,4,1152]{2,1,0:T(4,128)S(1)} collective-permute-done((f32[4,4,1152]{2,1,0:T(4,128)S(1)}, f32[4,4,1152]{2,1,0:T(4,128)S(1)}, u32[]{:S(2)}, u32[]{:S(2)}) %collective-permute-start.7) | collective-permute-done | bytes 73760 | tf_op jit(solution)/shard_map/ppermute | solution.py:41
  19.7 0.5 %collective-permute-done.8.refs_6_ = f32[4,4,1152]{2,1,0:T(4,128)S(1)} collective-permute-done((f32[4,4,1152]{2,1,0:T(4,128)S(1)}, f32[4,4,1152]{2,1,0:T(4,128)S(1)}, u32[]{:S(2)}, u32[]{:S(2)}) %collective-permute-start.8) | collective-permute-done | bytes 73760 | tf_op jit(solution)/shard_map/ppermute | solution.py:41
  20.3 2.9 %contract.1 = f32[4,2,2,4,1024]{4,3,2,1,0:T(4,128)S(1)} custom-call(f32[4,4,1152]{2,1,0:T(4,128)S(1)} %get-tuple-element.10.refs_0_, f32[4,4,1152]{2,1,0:T(4,128)S(1)} %collective-permute-done.3.refs_1_, f32[4,4,1152]{2,1,0:T(4,128)S(1)} %collective-permute-done.4.refs_2_, f32[4,4,1152]{2,1,0:T(4,128)S(1)} %collective-permute-done.5.refs_3_, ...), custom_call_target="tpu_custom_call" | custom-call | flops 805306368 | bytes 9175040 | tf_op jit(solution)/shard_map/contract/pallas_call | solution.py:166
  23.2 14.2 %all_to_all.5 = f32[16,4,1024]{2,1,0:T(4,128)S(1)} all-to-all(f32[16,4,1024]{2,1,0:T(4,128)S(1)} %bitcast.9), channel_id=1, replica_groups=mesh['outer'=4,'inner'=2,'core'=2,'ij'=2] {'outer','inner','core'}, dimensions={0} | all-to-all | bytes 524288 | tf_op jit(solution)/shard_map/all_to_all | solution.py:200
  37.3 0.7 %copy.7 = f32[4,16384]{1,0:T(4,128)} copy(f32[4,16384]{1,0:T(4,128)S(1)} %bitcast.11) | data formatting | bytes 524288
  (7 shorter events, 0.0 us)
Async XLA Ops:
  1.4 10.2 %copy-start = (f32[2,4,1152]{2,1,0:T(4,128)S(1)}, f32[2,4,1152]{2,1,0:T(4,128)}, u32[]{:S(2)}) copy-start(f32[2,4,1152]{2,1,0:T(4,128)} %pack.1.refs_0_) | copy-start | bytes 110596
  1.4 9.3 %collective-permute-start.2 = (f32[2,4,1152]{2,1,0:T(4,128)}, f32[2,4,1152]{2,1,0:T(4,128)S(1)}, u32[]{:S(2)}, u32[]{:S(2)}) collective-permute-start(f32[2,4,1152]{2,1,0:T(4,128)} %pack.1.refs_0_), channel_id=1, source_target_pairs={{0,24},{8,16},{16,8},{24,0},{1,25},{9,17},{17,9},{25,1},{2,26},{10... | collective-permute-start | bytes 110600 | tf_op jit(solution)/shard_map/ppermute | solution.py:41
  6.5 5.1 %collective-permute-start.1 = (f32[2,4,1152]{2,1,0:T(4,128)}, f32[2,4,1152]{2,1,0:T(4,128)S(1)}, u32[]{:S(2)}, u32[]{:S(2)}) collective-permute-start(f32[2,4,1152]{2,1,0:T(4,128)} %pack.1.refs_0_), channel_id=1, source_target_pairs={{0,16},{8,24},{16,0},{24,8},{1,17},{9,25},{17,1},{25,9},{2,18},{10... | collective-permute-start | bytes 110600 | tf_op jit(solution)/shard_map/ppermute | solution.py:41
  6.5 5.1 %collective-permute-start = (f32[2,4,1152]{2,1,0:T(4,128)}, f32[2,4,1152]{2,1,0:T(4,128)S(1)}, u32[]{:S(2)}, u32[]{:S(2)}) collective-permute-start(f32[2,4,1152]{2,1,0:T(4,128)} %pack.1.refs_0_), channel_id=1, source_target_pairs={{0,8},{8,0},{16,24},{24,16},{1,9},{9,1},{17,25},{25,17},{2,10},{10... | collective-permute-start | bytes 110600 | tf_op jit(solution)/shard_map/ppermute | solution.py:41
  10.7 9.6 %copy-start.1 = (f32[1024]{0:T(1024)S(1)}, f32[1024]{0:T(1024)}, u32[]{:S(2)}) copy-start(f32[1024]{0:T(1024)} %param.7) | copy-start | bytes 12292
  11.6 5.3 %collective-permute-start.5 = (f32[4,4,1152]{2,1,0:T(4,128)S(1)}, f32[4,4,1152]{2,1,0:T(4,128)S(1)}, u32[]{:S(2)}, u32[]{:S(2)}) collective-permute-start(f32[4,4,1152]{2,1,0:T(4,128)S(1)} %get-tuple-element.9), channel_id=1, source_target_pairs={{0,5},{1,4},{4,1},{5,0},{2,7},{3,6},{6,3},{7,2},{8,13},{9,12},{12,... | collective-permute-start | bytes 221192 | tf_op jit(solution)/shard_map/ppermute | solution.py:41
  14.1 4.4 %collective-permute-start.3 = (f32[4,4,1152]{2,1,0:T(4,128)S(1)}, f32[4,4,1152]{2,1,0:T(4,128)S(1)}, u32[]{:S(2)}, u32[]{:S(2)}) collective-permute-start(f32[4,4,1152]{2,1,0:T(4,128)S(1)} %get-tuple-element.9), channel_id=1, source_target_pairs={{0,1},{1,0},{4,5},{5,4},{2,3},{3,2},{6,7},{7,6},{8,9},{9,8},{12,13... | collective-permute-start | bytes 221192 | tf_op jit(solution)/shard_map/ppermute | solution.py:41
  14.7 4.4 %collective-permute-start.4 = (f32[4,4,1152]{2,1,0:T(4,128)S(1)}, f32[4,4,1152]{2,1,0:T(4,128)S(1)}, u32[]{:S(2)}, u32[]{:S(2)}) collective-permute-start(f32[4,4,1152]{2,1,0:T(4,128)S(1)} %get-tuple-element.10.refs_0_), channel_id=1, source_target_pairs={{0,4},{1,5},{4,0},{5,1},{2,6},{3,7},{6,2},{7,3},{8,12},{9,13},{12,... | collective-permute-start | bytes 221192 | tf_op jit(solution)/shard_map/ppermute | solution.py:41
  15.2 3.9 %collective-permute-start.6 = (f32[4,4,1152]{2,1,0:T(4,128)S(1)}, f32[4,4,1152]{2,1,0:T(4,128)S(1)}, u32[]{:S(2)}, u32[]{:S(2)}) collective-permute-start(f32[4,4,1152]{2,1,0:T(4,128)S(1)} %get-tuple-element.10.refs_0_), channel_id=1, source_target_pairs={{0,2},{2,0},{1,3},{3,1},{4,6},{6,4},{5,7},{7,5},{8,10},{10,8},{9,1... | collective-permute-start | bytes 221192 | tf_op jit(solution)/shard_map/ppermute | solution.py:41
  16.9 2.1 %collective-permute-start.9 = (f32[4,4,1152]{2,1,0:T(4,128)S(1)}, f32[4,4,1152]{2,1,0:T(4,128)S(1)}, u32[]{:S(2)}, u32[]{:S(2)}) collective-permute-start(f32[4,4,1152]{2,1,0:T(4,128)S(1)} %collective-permute-done.5.refs_3_), channel_id=1, source_target_pairs={{0,2},{2,0},{1,3},{3,1},{4,6},{6,4},{5,7},{7,5},{8,10},{10,8},{9,1... | collective-permute-start | bytes 221192 | tf_op jit(solution)/shard_map/ppermute | solution.py:41
  18.5 1.3 %collective-permute-start.7 = (f32[4,4,1152]{2,1,0:T(4,128)S(1)}, f32[4,4,1152]{2,1,0:T(4,128)S(1)}, u32[]{:S(2)}, u32[]{:S(2)}) collective-permute-start(f32[4,4,1152]{2,1,0:T(4,128)S(1)} %collective-permute-done.3.refs_1_), channel_id=1, source_target_pairs={{0,2},{2,0},{1,3},{3,1},{4,6},{6,4},{5,7},{7,5},{8,10},{10,8},{9,1... | collective-permute-start | bytes 221192 | tf_op jit(solution)/shard_map/ppermute | solution.py:41
  19.0 1.3 %collective-permute-start.8 = (f32[4,4,1152]{2,1,0:T(4,128)S(1)}, f32[4,4,1152]{2,1,0:T(4,128)S(1)}, u32[]{:S(2)}, u32[]{:S(2)}) collective-permute-start(f32[4,4,1152]{2,1,0:T(4,128)S(1)} %collective-permute-done.4.refs_2_), channel_id=1, source_target_pairs={{0,2},{2,0},{1,3},{3,1},{4,6},{6,4},{5,7},{7,5},{8,10},{10,8},{9,1... | collective-permute-start | bytes 221192 | tf_op jit(solution)/shard_map/ppermute | solution.py:41
